TPU v7x, 512 devices: a whole 4x4x16 slice. The times are simulated.
512 devices in a mesh: grp: 16 (over y, x), tp: 32 (over z, core).
Axes of the slice: x: 4, y: 4, z: 16, core: 2. Of those that a mesh axis runs over, the one named last changes fastest.
Arguments:
- tokens: bfloat16 [6144, 5120], P('grp'), may hold values from -36 to 36
- trainer_panels: bfloat16 [64, 5120, 128], P('tp', 'grp'), may hold values from -0.078125 to 0.078125
- panel_home: int32 [48], replicated, may hold values from 0 to 63, as said below
- lengths: int32 [16, 4], P('grp'), may hold values from 1 to 192, 384 in all within a row
Outputs:
- context: float32 [6144, 4096], P(('grp', 'tp'))
Inputs may be any that keep to these rules, and one draw needn't show every extreme that they name: `panel_home`: entries are distinct; entry p is 2 times the tp index of the trainer device that holds panel p, plus the panel's slot on that device. Panels 0 to 31 are query heads, the next 8 key heads, the last 8 value heads. Some trainer device holds 2 panels.
All inputs are finite; a program needn't handle non-finite values.
Results may differ from a plain program's by a relative error of at most 0.012.
Values may be sent and summed in bfloat16 or wider, within the bound.
A program may use at most 64 MiB of HBM per device.

v0:
```python
import jax
import jax.numpy as jnp
from jax import lax
from jax.sharding import PartitionSpec as P


def on_device(tokens, trainer_panels, panel_home, lengths):
    tp_count = lax.axis_size("tp")
    grp_count = lax.axis_size("grp")
    member_id = lax.axis_index("tp")
    kv_count = (panel_home.shape[0] - tp_count) // 2
    group_size = tp_count // kv_count
    head_dim = trainer_panels.shape[2]
    block_rows = trainer_panels.shape[1]
    half_rows = block_rows // 2
    seq_total = tokens.shape[0]
    all_slots = lax.all_gather(trainer_panels, "tp", axis=0, tiled=True)
    kv_id = member_id // group_size
    quarter = member_id % group_size
    kv_panel = tp_count + kv_id + kv_count * (quarter // 2)
    half = quarter % 2
    q_block = all_slots[panel_home[member_id]]
    kv_block = all_slots[panel_home[kv_panel]]
    kv_half = lax.dynamic_slice_in_dim(kv_block, half * half_rows, half_rows, axis=0)
    piece = jnp.concatenate([q_block, kv_half], axis=0)
    gathered = lax.all_gather(piece, "grp", axis=0, tiled=False)
    q_weights = gathered[:, :block_rows].reshape(grp_count * block_rows, head_dim)
    kv_weights = gathered[:, block_rows:]
    query_rows = jnp.dot(tokens, q_weights, preferred_element_type=jnp.float32).astype(jnp.bfloat16)
    token_halves = tokens.reshape(seq_total, grp_count, 2, half_rows)
    token_half = lax.dynamic_index_in_dim(token_halves, half, axis=2, keepdims=False)
    kv_part = jnp.einsum("sgi,gic->sc", token_half, kv_weights, preferred_element_type=jnp.float32)
    pair_perm = [(i, i ^ 1) for i in range(tp_count)]
    kv_full = (kv_part + lax.ppermute(kv_part, "tp", pair_perm)).astype(jnp.bfloat16)
    swap_perm = [(i, i ^ 2) for i in range(tp_count)]
    kv_other = lax.ppermute(kv_full, "tp", swap_perm)
    holds_k = quarter < 2
    key_rows = jnp.where(holds_k, kv_full, kv_other)
    value_rows = jnp.where(holds_k, kv_other, kv_full)
    position = jnp.arange(seq_total, dtype=jnp.int32)
    bounds = jnp.cumsum(lengths[0])
    segment = jnp.sum((position[:, None] >= bounds[None, :]).astype(jnp.int32), axis=1)
    allowed = (segment[:, None] == segment[None, :]) & (position[None, :] <= position[:, None])
    score_scale = head_dim ** (-0.5)
    scores = (
        lax.dot_general(
            query_rows, key_rows, (((1,), (1,)), ((), ())), preferred_element_type=jnp.float32
        )
        * score_scale
    )
    masked = jnp.where(allowed, scores, -jnp.inf)
    row_peak = jnp.max(masked, axis=1, keepdims=True)
    row_exp = jnp.exp(masked - row_peak)
    attn_probs = (row_exp / jnp.sum(row_exp, axis=1, keepdims=True)).astype(jnp.bfloat16)
    context = jnp.dot(attn_probs, value_rows, preferred_element_type=jnp.float32)
    return lax.all_to_all(context, "tp", split_axis=0, concat_axis=1, tiled=True)


def solution(mesh):
    placed = (P("grp", None), P("tp", "grp", None), P(), P("grp", None))
    return jax.shard_map(
        on_device, mesh=mesh, in_specs=placed, out_specs=P(("grp", "tp"), None), check_vma=False
    )
```

profile of v0, /device:TPU:1, one launch (start us, length us, event | category | flops | bytes accessed | tf_op | source)
XLA Modules:
  0.0 209.4 jit_solution(2811401276876923710)
XLA Ops:
  6.5 0.7 all-gather.4.cloned.1.call-update
  7.3 0.0 all-gather.6.cloned.1.call-start
  7.4 1.4 fusion.16
  12.6 78.4 %all-gather.4.cloned.1.call-done = bf16[64,320,128]{2,1,0:T(8,128)(2,1)} async-done(((bf16[2,320,128]{2,1,0:T(8,128)(2,1)}), bf16[64,320,128]{2,1,0:T(8,128)(2,1)}) %all-gather.4.cloned.1.call-update) | async-done | bytes 5242896 | tf_op jit(solution)/shard_map/all_gather | solution.py:17
  91.0 0.9 dynamic-slice_bitcast_fusion
  91.9 0.8 dynamic-slice_bitcast_fusion.1
  92.7 0.7 pad_maximum_fusion
  93.3 0.0 all-gather.6.cloned.1.call-update
  93.4 6.3 %copy.12 = bf16[384,5120]{0,1:T(8,128)(2,1)} copy(bf16[384,5120]{1,0:T(8,128)(2,1)} %param.4) | data formatting | bytes 7864320 | tf_op args[0]
  99.6 49.6 %all-gather.6.cloned.1.call-done = bf16[7680,128]{1,0:T(8,128)(2,1)} async-done(((bf16[480,128]{1,0:T(8,128)(2,1)}), bf16[7680,128]{1,0:T(8,128)(2,1)}) %all-gather.6.cloned.1.call-update) | async-done | bytes 1966096 | tf_op jit(solution)/shard_map/all_gather | solution.py:26
  149.2 2.5 %fusion.4 = f32[384,128]{1,0:T(8,128)S(1)} fusion(bf16[384,16,2,160]{0,3,2,1:T(8,128)(2,1)} %bitcast.25, s32[]{:T(128)S(6)} %select_n.69, bf16[16,480,128]{2,1,0:T(8,128)(2,1)} %bitcast.28), kind=kOutput, calls=%fused_computation.5 | convolution fusion | flops 251658240 | bytes 2818052 | tf_op jit(solution)/shard_map/sgi,gic->sc/dot_general | solution.py:32
  151.8 3.4 %collective-permute-start = (f32[384,128]{1,0:T(8,128)S(1)}, f32[384,128]{1,0:T(8,128)S(1)}, u32[]{:S(2)}, u32[]{:S(2)}) collective-permute-start(f32[384,128]{1,0:T(8,128)S(1)} %fusion.4), channel_id=1, source_target_pairs={{0,1},{1,0},{2,3},{3,2},{4,5},{5,4},{6,7},{7,6},{8,9},{9,8},{10,11... | collective-permute-start | bytes 589832 | tf_op jit(solution)/shard_map/ppermute | solution.py:34
  155.2 0.2 reduce-window.8
  155.3 0.9 collective-permute-done
  156.2 3.2 %collective-permute-start.1 = (bf16[384,128]{1,0:T(8,128)(2,1)S(1)}, bf16[384,128]{1,0:T(8,128)(2,1)S(1)}, u32[]{:S(2)}, u32[]{:S(2)}) collective-permute-start(bf16[384,128]{1,0:T(8,128)(2,1)S(1)} %add_convert_fusion), channel_id=1, source_target_pairs={{0,2},{1,3},{2,0},{3,1},{4,6},{5,7},{6,4},{7,5},{8,10},{9,11},{10,... | collective-permute-start | bytes 294920 | tf_op jit(solution)/shard_map/ppermute | solution.py:36
  159.4 0.1 convert_reduce_fusion
  159.5 0.1 slice.9
  159.6 2.5 %collective-permute-done.1 = bf16[384,128]{1,0:T(8,128)(2,1)S(1)} collective-permute-done((bf16[384,128]{1,0:T(8,128)(2,1)S(1)}, bf16[384,128]{1,0:T(8,128)(2,1)S(1)}, u32[]{:S(2)}, u32[]{:S(2)}) %collective-permute-start.1) | collective-permute-done | bytes 98336 | tf_op jit(solution)/shard_map/ppermute | solution.py:36
  162.1 3.7 %fusion.17 = (f32[384]{0:T(512)S(1)}, f32[384,384]{0,1:T(8,128)S(1)}) fusion(bf16[5120,128]{1,0:T(8,128)(2,1)S(1)} %bitcast.24, bf16[384,5120]{1,0:T(8,128)(2,1)} %param.4, bf16[384,128]{1,0:T(8,128)(2,1)S(1)} %add_convert_fusion, bf16[384,128]{1,0:T(8,128)(2,1)S(1)} %collective-permute-done.1, pred[]{:T(512)S(6)} %lt.39, s32[384]{0:T(512)S(1)} %convert_reduce_fusion), kind=kOutput, calls=%fused_computation.26 | convolution fusion | flops 542047872 | bytes 6032385 | tf_op jit(solution)/shard_map/dot_general | solution.py:46
  165.9 0.1 fusion.9
  166.0 0.3 fusion.10
  166.3 35.3 %all_to_all.19 = f32[32,12,128]{2,1,0:T(8,128)S(1)} all-to-all(f32[32,12,128]{2,1,0:T(8,128)S(1)} %all_to_all.14), channel_id=1, replica_groups=mesh['grp'=16,'tp'=32] {'tp'}, dimensions={0} | all-to-all | bytes 393216 | tf_op jit(solution)/shard_map/all_to_all | solution.py:56
  201.7 0.1 copy.13
  201.8 0.9 copy.14
  (8 shorter events, 0.1 us)
Async XLA Ops:
  6.5 84.4 %all-gather.4.cloned.1.call-start = ((), (), s32[]{:S(2)}) async-start(), calls=%async_computation.1 | async-start | bytes 5406720 | tf_op jit(solution)/shard_map/all_gather | solution.py:17
  7.3 142.0 %all-gather.6.cloned.1.call-start = ((), (), s32[]{:S(2)}) async-start(), calls=%async_computation.2 | async-start | bytes 2088960 | tf_op jit(solution)/shard_map/all_gather | solution.py:26
  93.4 61.8 %copy-start.1 = (s32[1,4]{1,0:T(1,128)S(1)}, s32[1,4]{1,0:T(1,128)}, u32[]{:S(2)}) copy-start(s32[1,4]{1,0:T(1,128)} %param.7) | copy-start | bytes 52
  149.2 10.3 %copy-start = (bf16[7680,128]{1,0:T(8,128)(2,1)S(1)}, bf16[7680,128]{1,0:T(8,128)(2,1)}, u32[]{:S(2)}) copy-start(bf16[7680,128]{1,0:T(8,128)(2,1)} %all-gather.6.cloned.1.call-done) | copy-start | bytes 5898244
  151.8 4.4 %collective-permute-start = (f32[384,128]{1,0:T(8,128)S(1)}, f32[384,128]{1,0:T(8,128)S(1)}, u32[]{:S(2)}, u32[]{:S(2)}) collective-permute-start(f32[384,128]{1,0:T(8,128)S(1)} %fusion.4), channel_id=1, source_target_pairs={{0,1},{1,0},{2,3},{3,2},{4,5},{5,4},{6,7},{7,6},{8,9},{9,8},{10,11... | collective-permute-start | bytes 589832 | tf_op jit(solution)/shard_map/ppermute | solution.py:34
  156.2 5.9 %collective-permute-start.1 = (bf16[384,128]{1,0:T(8,128)(2,1)S(1)}, bf16[384,128]{1,0:T(8,128)(2,1)S(1)}, u32[]{:S(2)}, u32[]{:S(2)}) collective-permute-start(bf16[384,128]{1,0:T(8,128)(2,1)S(1)} %add_convert_fusion), channel_id=1, source_target_pairs={{0,2},{1,3},{2,0},{3,1},{4,6},{5,7},{6,4},{7,5},{8,10},{9,11},{10,... | collective-permute-start | bytes 294920 | tf_op jit(solution)/shard_map/ppermute | solution.py:36
Sparse Core Ops, SparseCore 0:
  9.5 81.4 all-gather.3
  94.0 55.1 all-gather.5
where the time goes:
time: 210 us; the launch traced here: 209 us
  waiting for transfers between devices  132 us (63%)
  blocking collectives  35.3 us (17%)
  between operations  17.4 us (8%)
  local copies, waits for them, and re-layouts  10.4 us (5%)
  starting transfers between devices  6.58 us (3%)
  matrix products  6.57 us (3%)
    all_gather x1, waiting for transfers between devices, on_device(): all_slots = lax.all_gather(trainer_panels, 'tp', axis=0, tiled=True)  78.4 us
    all_gather x1, waiting for transfers between devices, on_device(): gathered = lax.all_gather(piece, 'grp', axis=0, tiled=False)  49.6 us
    all_to_all x1, blocking collectives, on_device(): lax.all_to_all(context, 'tp', split_axis=0, concat_axis=1, tiled=True)  35.3 us
    unnamed x7, local copies, waits for them, and re-layouts  7.16 us
  transfers between devices with their start and end apart: 4, of which 4 were waited for; matrix products, arithmetic and copies ran while one was open for 4% of the time, Pallas kernels for 0%

commit v1 on v0

--- a/solution.py
+++ b/solution.py
@@ -14,7 +14,9 @@
     block_rows = trainer_panels.shape[1]
     half_rows = block_rows // 2
     seq_total = tokens.shape[0]
-    all_slots = lax.all_gather(trainer_panels, "tp", axis=0, tiled=True)
+    all_slots = jnp.concatenate(
+        lax.all_to_all(jnp.stack([trainer_panels] * lax.axis_size("tp")), "tp", 0, 0), axis=0
+    )
     kv_id = member_id // group_size
     quarter = member_id % group_size
     kv_panel = tp_count + kv_id + kv_count * (quarter // 2)

time: 210 us -> 378 us (1.80)
  waiting for transfers between devices: 132 us -> 279 us
  starting transfers between devices: 6.58 us -> 23.5 us
  local copies, waits for them, and re-layouts: 10.4 us -> 14.2 us
    all_to_all x0 -> x1, waiting for transfers between devices: none -> 228 us  [on_device(): lax.all_to_all(jnp.stack([trainer_panels] * lax.axis_size('tp')), 'tp', 0...]
    all_gather x1 -> x0, waiting for transfers between devices: 78.4 us -> none  [on_device(): all_slots = lax.all_gather(trainer_panels, 'tp', axis=0, tiled=True)]
    all_to_all x0 -> x1, starting transfers between devices: none -> 16.9 us  [on_device(): lax.all_to_all(jnp.stack([trainer_panels] * lax.axis_size('tp')), 'tp', 0...]
    another operation x0 -> x1, local copies, waits for them, and re-layouts: none -> 4.53 us  [on_device(): jnp.stack([trainer_panels] * lax.axis_size('tp'))]
  transfers between devices with their start and end apart: 4 -> 4, of which waited for: 4 -> 4; matrix products, arithmetic and copies ran while one was open for 4% -> 2% of each run, Pallas kernels for 0% -> 0%
where the time goes in v1:
time: 378 us; the launch traced here: 377 us
  waiting for transfers between devices  279 us (74%)
  blocking collectives  35.3 us (9%)
  starting transfers between devices  23.5 us (6%)
  between operations  17.2 us (5%)
  local copies, waits for them, and re-layouts  14.2 us (4%)
  matrix products  6.52 us (2%)
    all_to_all x1, waiting for transfers between devices, on_device(): lax.all_to_all(jnp.stack([trainer_panels] * lax.axis_size('tp')), 'tp', 0...  228 us
    all_gather x1, waiting for transfers between devices, on_device(): gathered = lax.all_gather(piece, 'grp', axis=0, tiled=False)  48.3 us
    all_to_all x1, blocking collectives, on_device(): lax.all_to_all(context, 'tp', split_axis=0, concat_axis=1, tiled=True)  35.3 us
    all_to_all x1, starting transfers between devices, on_device(): lax.all_to_all(jnp.stack([trainer_panels] * lax.axis_size('tp')), 'tp', 0...  16.9 us
  transfers between devices with their start and end apart: 4, of which 4 were waited for; matrix products, arithmetic and copies ran while one was open for 2% of the time, Pallas kernels for 0%

profile of v1, /device:TPU:1, one launch (start us, length us, event | category | flops | bytes accessed | tf_op | source)
XLA Modules:
  0.0 377.0 jit_solution(17143165539301071188)
XLA Ops:
  6.5 4.5 %stack.2 = bf16[32,2,320,128]{3,2,1,0:T(8,128)(2,1)} broadcast(bf16[2,320,128]{2,1,0:T(8,128)(2,1)} %param.5), dimensions={1,2,3} | broadcast | bytes 5406720 | tf_op jit(solution)/shard_map/stack | solution.py:18
  11.1 16.9 %all-to-all-start = ((bf16[32,2,320,128]{3,2,1,0:T(8,128)(2,1)}), bf16[32,2,320,128]{3,2,1,0:T(8,128)(2,1)}, u32[]{:S(2)}, u32[]{:S(2)}) async-start(bf16[32,2,320,128]{3,2,1,0:T(8,128)(2,1)} %stack.2), calls=%async_computation | async-start | bytes 10485760 | tf_op jit(solution)/shard_map/all_to_all | solution.py:18
  28.0 0.0 all-gather.3.cloned.1.call-start
  28.1 0.6 fusion.16
  32.3 227.5 %all-to-all-done = bf16[32,2,320,128]{3,2,1,0:T(8,128)(2,1)} async-done(((bf16[32,2,320,128]{3,2,1,0:T(8,128)(2,1)}), bf16[32,2,320,128]{3,2,1,0:T(8,128)(2,1)}, u32[]{:S(2)}, u32[]{:S(2)}) %all-to-all-start) | async-done | bytes 5242912 | tf_op jit(solution)/shard_map/all_to_all | solution.py:18
  259.8 0.9 dynamic-slice_bitcast_fusion
  260.7 0.8 dynamic-slice_bitcast_fusion.1
  261.5 0.7 pad_maximum_fusion
  262.2 6.3 %copy.10 = bf16[384,5120]{0,1:T(8,128)(2,1)} copy(bf16[384,5120]{1,0:T(8,128)(2,1)} %param.4) | data formatting | bytes 7864320 | tf_op args[0]
  268.5 48.3 %all-gather.3.cloned.1.call-done = bf16[7680,128]{1,0:T(8,128)(2,1)} async-done(((bf16[480,128]{1,0:T(8,128)(2,1)}), bf16[7680,128]{1,0:T(8,128)(2,1)}) %all-gather.3.cloned.1.call-update) | async-done | bytes 1966096 | tf_op jit(solution)/shard_map/all_gather | solution.py:28
  316.8 2.5 fusion.4
  319.4 3.4 collective-permute-start
  322.8 0.2 reduce-window.8
  322.9 0.9 collective-permute-done
  323.8 3.2 collective-permute-start.1
  327.0 0.1 convert_reduce_fusion
  327.1 0.1 slice.9
  327.2 2.5 collective-permute-done.1
  329.7 3.7 fusion.17
  333.4 0.1 fusion.9
  333.5 0.3 fusion.10
  333.9 35.3 %all_to_all.24 = f32[32,12,128]{2,1,0:T(8,128)S(1)} all-to-all(f32[32,12,128]{2,1,0:T(8,128)S(1)} %all_to_all.18), channel_id=1, replica_groups=mesh['grp'=16,'tp'=32] {'tp'}, dimensions={0} | all-to-all | bytes 393216 | tf_op jit(solution)/shard_map/all_to_all | solution.py:58
  369.2 0.1 copy.11
  369.3 0.9 copy.12
  (10 shorter events, 0.1 us)
Async XLA Ops:
  11.1 17.0 %copy-start.1 = (s32[48]{0:T(128)S(1)}, s32[48]{0:T(128)}, u32[]{:S(2)}) copy-start(s32[48]{0:T(128)} %param.6) | copy-start | bytes 580
  11.1 248.8 %all-to-all-start = ((bf16[32,2,320,128]{3,2,1,0:T(8,128)(2,1)}), bf16[32,2,320,128]{3,2,1,0:T(8,128)(2,1)}, u32[]{:S(2)}, u32[]{:S(2)}) async-start(bf16[32,2,320,128]{3,2,1,0:T(8,128)(2,1)} %stack.2), calls=%async_computation | async-start | bytes 10485760 | tf_op jit(solution)/shard_map/all_to_all | solution.py:18
  28.0 288.8 %all-gather.3.cloned.1.call-start = ((), (), s32[]{:S(2)}) async-start(), calls=%async_computation.2 | async-start | bytes 2088960 | tf_op jit(solution)/shard_map/all_gather | solution.py:28
  262.2 60.5 %copy-start.2 = (s32[1,4]{1,0:T(1,128)S(1)}, s32[1,4]{1,0:T(1,128)}, u32[]{:S(2)}) copy-start(s32[1,4]{1,0:T(1,128)} %param.7) | copy-start | bytes 52
  316.8 10.3 %copy-start = (bf16[7680,128]{1,0:T(8,128)(2,1)S(1)}, bf16[7680,128]{1,0:T(8,128)(2,1)}, u32[]{:S(2)}) copy-start(bf16[7680,128]{1,0:T(8,128)(2,1)} %all-gather.3.cloned.1.call-done) | copy-start | bytes 5898244
  319.4 4.4 %collective-permute-start = (f32[384,128]{1,0:T(8,128)S(1)}, f32[384,128]{1,0:T(8,128)S(1)}, u32[]{:S(2)}, u32[]{:S(2)}) collective-permute-start(f32[384,128]{1,0:T(8,128)S(1)} %fusion.4), channel_id=1, source_target_pairs={{0,1},{1,0},{2,3},{3,2},{4,5},{5,4},{6,7},{7,6},{8,9},{9,8},{10,11... | collective-permute-start | bytes 589832 | tf_op jit(solution)/shard_map/ppermute | solution.py:36
  323.8 5.9 %collective-permute-start.1 = (bf16[384,128]{1,0:T(8,128)(2,1)S(1)}, bf16[384,128]{1,0:T(8,128)(2,1)S(1)}, u32[]{:S(2)}, u32[]{:S(2)}) collective-permute-start(bf16[384,128]{1,0:T(8,128)(2,1)S(1)} %add_convert_fusion), channel_id=1, source_target_pairs={{0,2},{1,3},{2,0},{3,1},{4,6},{5,7},{6,4},{7,5},{8,10},{9,11},{10,... | collective-permute-start | bytes 294920 | tf_op jit(solution)/shard_map/ppermute | solution.py:38
Sparse Core Ops, SparseCore 0:
  262.3 54.4 all-gather.2
